TPU v7x, 256 devices: a whole 4x4x8 slice. The times are simulated.
256 devices in a mesh: layer: 2 (over core), ex: 128 (over z, y, x).
Axes of the slice: x: 4, y: 4, z: 8, core: 2. Of those that a mesh axis runs over, the one named last changes fastest.
Arguments:
- train_sketch: bfloat16 [12, 65536, 256], P('layer', 'ex')
- val_sketch: bfloat16 [12, 4096, 256], P('layer', 'ex')
- first_moment: float32 [12, 256], P('layer'), may hold values from -0.6 to 0.6
- second_moment: float32 [12, 256], P('layer'), may hold values from 0.01 to 1
- train_pair: int32 [65536], P('ex'), may hold values from 0 to 15
- val_pair: int32 [4096], P('ex'), may hold values from 0 to 15
- block_mask: int32 [16, 16], replicated, may hold values 0 or 1
Outputs:
- scores: bfloat16 [32768, 2, 4096], P('ex', 'layer')
All inputs are finite; a program needn't handle non-finite values.
Results may differ from a plain program's by a relative error of at most 0.0058.
Values may be sent and summed in bfloat16 or wider, within the bound.
No kernel may reach another device: no remote copies, remote signals or barrier semaphores. Data moves between devices by JAX's collectives and lax.ppermute only.
A program may use at most 128 MiB of HBM per device.

v0:
```python
import jax
import jax.numpy as jnp
from jax import lax
from jax.sharding import PartitionSpec as P


def precondition(grad, first_moment, second_moment):
    return (0.9 * first_moment[:, None, :] + 0.1 * grad) / (
        jnp.sqrt(0.999 * second_moment[:, None, :] + 0.001 * grad * grad) + 1e-08
    )


def squares(values):
    return jnp.sum(values * values, axis=(0, 2))


def unit_rows(values, total_sq, scale_factor):
    return (values * (scale_factor * lax.rsqrt(total_sq + 1e-06))[None, :, None]).astype(
        jnp.bfloat16
    )


def contract(left, right):
    return lax.dot_general(
        left, right, (((0, 2), (0, 2)), ((), ())), preferred_element_type=jnp.float32
    )


def local(train_sketch, val_sketch, first_moment, second_moment, train_pair, val_pair, block_mask):
    lay_dev, tr_ex, width = train_sketch.shape
    layer_count = lax.axis_size("layer")
    rows_here = tr_ex // layer_count
    scale_factor = float(lay_dev * layer_count * width) ** 0.25
    pair_count = block_mask.shape[0]
    labels = jnp.arange(pair_count, dtype=jnp.int32)
    val_all = lax.all_gather(val_sketch, "ex", axis=1, tiled=True)
    val_labels = lax.all_gather(val_pair, "ex", axis=0, tiled=True)
    val_onehot = (labels[:, None] == val_labels[None, :]).astype(jnp.bfloat16)
    pairs_here = lax.dynamic_slice_in_dim(
        train_pair, lax.axis_index("layer") * rows_here, rows_here, 0
    )
    mine = lax.all_to_all(train_sketch, "layer", split_axis=1, concat_axis=0, tiled=True)
    first_all, second_all = (
        lax.all_gather(first_moment, "layer", axis=0, tiled=True),
        lax.all_gather(second_moment, "layer", axis=0, tiled=True),
    )
    val_full = lax.all_gather(val_all, "layer", axis=0, tiled=True)
    pre = precondition(mine.astype(jnp.float32), first_all, second_all)
    unit_train = unit_rows(pre, squares(pre), scale_factor)
    val_float = val_full.astype(jnp.float32)
    unit_val = unit_rows(val_float, squares(val_float), scale_factor)
    raw = contract(unit_train, unit_val)
    train_onehot = (pairs_here[:, None] == labels[None, :]).astype(jnp.bfloat16)
    row_mask = jnp.dot(
        train_onehot, block_mask.astype(jnp.bfloat16), preferred_element_type=jnp.float32
    ).astype(jnp.bfloat16)
    weights = jnp.dot(row_mask, val_onehot, preferred_element_type=jnp.float32)
    return (raw * weights).astype(jnp.bfloat16)[:, None, :]


def solution(mesh):
    placed = (
        P("layer", "ex", None),
        P("layer", "ex", None),
        P("layer", None),
        P("layer", None),
        P("ex"),
        P("ex"),
        P(),
    )
    return jax.shard_map(
        local, mesh=mesh, in_specs=placed, out_specs=P("ex", "layer", None), check_vma=False
    )
```

profile of v0, /device:TPU:0, one launch (start us, length us, event | category | flops | bytes accessed | tf_op | source)
XLA Modules:
  0.0 894.7 jit_solution(7352749476020731532)
XLA Ops:
  6.5 0.7 all-gather.5.cloned.1.call-update
  7.3 0.0 all-gather.7.cloned.1.call-start
  7.3 143.9 %all-gather.5.cloned.1.call-done = bf16[6,4096,256]{2,1,0:T(8,128)(2,1)} async-done(((bf16[6,32,256]{2,1,0:T(8,128)(2,1)}), bf16[6,4096,256]{2,1,0:T(8,128)(2,1)}) %all-gather.5.cloned.1.call-update) | async-done | bytes 12582928 | tf_op jit(solution)/shard_map/all_gather | solution.py:36
  151.2 0.0 all-gather.7.cloned.1.call-update
  151.2 1.4 copy-done
  152.6 2.2 copy.14
  154.9 3.8 all-to-all-start
  158.6 2.6 all-gather
  161.3 1.8 all-gather.1
  163.1 0.3 convert_bitcast_fusion
  163.5 0.0 copy-start.6
  163.5 0.0 copy-start.4
  163.5 0.0 copy-start.5
  163.5 3.4 copy.15
  166.9 0.6 dynamic-slice
  168.1 0.1 dynamic_slice.3
  168.2 0.2 dynamic-update-slice
  168.5 684.9 %all-reduce = s32[4096]{0:T(1024)S(1)} all-reduce(s32[4096]{0:T(1024)S(1)} %dynamic-update-slice), channel_id=1, replica_groups=mesh['layer'=2,'ex'=128] {'ex'}, use_global_device_ids=true, to_apply=%add | all-reduce | flops 4096 | bytes 32768
  853.4 2.9 fusion.15
  856.3 3.6 fusion.22
  859.9 0.0 all-gather.7.cloned.1.call-done
  859.9 10.3 %fusion = f32[4096]{0:T(1024)S(1)} fusion(bf16[12,4096,256]{2,1,0:T(8,128)(2,1)} %all-gather.7.cloned.1.call-done), kind=kLoop, calls=%fused_computation.2 | loop fusion | flops 37744640 | bytes 25182208 | tf_op jit(solution)/shard_map/reduce_sum | solution.py:14
  870.3 13.1 %fusion.5 = f32[256,4096]{1,0:T(8,128)} fusion(bf16[12,256,256]{2,1,0:T(8,128)(2,1)S(1)} %fusion.22, bf16[12,4096,256]{2,1,0:T(8,128)(2,1)} %all-gather.7.cloned.1.call-done, f32[4096]{0:T(1024)S(1)} %rsqrt_multiply_fusion), kind=kOutput, calls=%fused_computation.7 | convolution fusion | flops 6480199680 | bytes 30949376 | tf_op jit(solution)/shard_map/dot_general | solution.py:24
  883.4 4.5 fusion.9
  (19 shorter events, 0.1 us)
Async XLA Ops:
  6.5 144.7 %all-gather.5.cloned.1.call-start = ((), (), s32[]{:S(2)}) async-start(), calls=%async_computation.1 | async-start | bytes 12681216 | tf_op jit(solution)/shard_map/all_gather | solution.py:36
  7.3 852.7 %all-gather.7.cloned.1.call-start = ((), (), s32[]{:S(2)}) async-start(), calls=%async_computation.2 | async-start | bytes 37748736 | tf_op jit(solution)/shard_map/all_gather | solution.py:47
  151.2 1.4 copy-start
  152.6 6.0 copy-start.2
  152.6 8.7 copy-start.3
  154.9 8.3 all-to-all-start
  163.5 3.4 copy-start.6
  163.5 4.7 copy-start.4
  163.5 4.7 copy-start.5
  870.3 13.1 %copy-start.1 = (s32[16,16]{1,0:T(8,128)S(1)}, s32[16,16]{1,0:T(8,128)}, u32[]{:S(2)}) copy-start(s32[16,16]{1,0:T(8,128)} %param.13) | copy-start | bytes 3076
Sparse Core Ops, SparseCore 0:
  10.9 140.2 all-gather.4
  153.0 42.9 all-gather.6
where the time goes:
time: 895 us
  blocking collectives  689 us (77%)
  waiting for transfers between devices  145 us (16%)
  matrix products  17.6 us (2%)
  other arithmetic  17.2 us (2%)
  between operations  14.2 us (2%)
    unnamed x1, blocking collectives  685 us
    all_gather x1, waiting for transfers between devices, local(): val_all = lax.all_gather(val_sketch, 'ex', axis=1, tiled=True)  144 us
  transfers between devices with their start and end apart: 3, of which 1 were waited for; matrix products, arithmetic and copies ran while one was open for 1% of the time, Pallas kernels for 0%

commit v1 on v0

--- a/solution.py
+++ b/solution.py
@@ -33,7 +33,9 @@
     scale_factor = float(lay_dev * layer_count * width) ** 0.25
     pair_count = block_mask.shape[0]
     labels = jnp.arange(pair_count, dtype=jnp.int32)
-    val_all = lax.all_gather(val_sketch, "ex", axis=1, tiled=True)
+    val_all = jnp.concatenate(
+        lax.all_to_all(jnp.stack([val_sketch] * lax.axis_size("ex")), "ex", 0, 0), axis=1
+    )
     val_labels = lax.all_gather(val_pair, "ex", axis=0, tiled=True)
     val_onehot = (labels[:, None] == val_labels[None, :]).astype(jnp.bfloat16)
     pairs_here = lax.dynamic_slice_in_dim(

time: 895 us -> 1050 us (1.17)
  blocking collectives: 689 us -> 979 us
  waiting for transfers between devices: 145 us -> 2.88 us
  local copies, waits for them, and re-layouts: 7.94 us -> 20.2 us
    all_to_all x0 -> x1, blocking collectives: none -> 290 us  [local(): lax.all_to_all(jnp.stack([val_sketch] * lax.axis_size('ex')), 'ex', 0, 0)]
    all_gather x1 -> x0, waiting for transfers between devices: 144 us -> none  [local(): val_all = lax.all_gather(val_sketch, 'ex', axis=1, tiled=True)]
  transfers between devices with their start and end apart: 3 -> 2, of which waited for: 1 -> 1; matrix products, arithmetic and copies ran while one was open for 1% -> 1% of each run, Pallas kernels for 0% -> 0%
where the time goes in v1:
time: 1050 us
  blocking collectives  979 us (93%)
  local copies, waits for them, and re-layouts  20.2 us (2%)
  matrix products  17.5 us (2%)
  other arithmetic  17.2 us (2%)
  between operations  14.2 us (1%)
    unnamed x1, blocking collectives  685 us
    all_to_all x1, blocking collectives, local(): lax.all_to_all(jnp.stack([val_sketch] * lax.axis_size('ex')), 'ex', 0, 0)  290 us
  transfers between devices with their start and end apart: 2, of which 1 were waited for; matrix products, arithmetic and copies ran while one was open for 1% of the time, Pallas kernels for 0%

profile of v1, /device:TPU:0, one launch (start us, length us, event | category | flops | bytes accessed | tf_op | source)
XLA Modules:
  0.0 1054.5 jit_solution(16616266552468745484)
XLA Ops:
  6.5 7.0 stack.2
  13.6 289.9 %all_to_all.14 = bf16[128,6,32,256]{3,2,1,0:T(8,128)(2,1)S(1)} all-to-all(bf16[128,6,32,256]{3,2,1,0:T(8,128)(2,1)} %stack.2), channel_id=1, replica_groups=mesh['layer'=2,'ex'=128] {'ex'}, dimensions={0} | all-to-all | bytes 25165824 | tf_op jit(solution)/shard_map/all_to_all | solution.py:37
  303.5 5.2 copy.18
  308.7 0.0 all-gather.4.cloned.1.call-update
  308.8 1.4 copy-done
  310.1 2.2 copy.16
  312.4 3.8 all-to-all-start
  316.2 2.8 all-to-all-done
  319.0 0.3 convert_bitcast_fusion
  319.3 0.0 copy-start.2
  319.4 0.0 copy-start.6
  319.4 3.3 copy.17
  322.7 1.8 all-gather.1
  324.5 1.8 all-gather
  326.4 0.6 dynamic-slice
  327.6 0.1 dynamic_slice.3
  327.7 0.2 dynamic-update-slice
  327.9 685.4 %all-reduce = s32[4096]{0:T(1024)S(1)} all-reduce(s32[4096]{0:T(1024)S(1)} %dynamic-update-slice), channel_id=1, replica_groups=mesh['layer'=2,'ex'=128] {'ex'}, use_global_device_ids=true, to_apply=%add | all-reduce | flops 4096 | bytes 32768
  1013.3 2.9 fusion.15
  1016.2 3.6 fusion.22
  1019.8 0.0 all-gather.4.cloned.1.call-done
  1019.8 10.3 fusion
  1030.2 13.0 %fusion.5 = f32[256,4096]{1,0:T(8,128)} fusion(bf16[12,256,256]{2,1,0:T(8,128)(2,1)S(1)} %fusion.22, bf16[12,4096,256]{2,1,0:T(8,128)(2,1)} %all-gather.4.cloned.1.call-done, f32[4096]{0:T(1024)S(1)} %rsqrt_multiply_fusion), kind=kOutput, calls=%fused_computation.7 | convolution fusion | flops 6480199680 | bytes 30949376 | tf_op jit(solution)/shard_map/dot_general | solution.py:24
  1043.2 4.5 fusion.9
  (19 shorter events, 0.1 us)
Async XLA Ops:
  6.5 1013.3 %all-gather.4.cloned.1.call-start = ((), (), s32[]{:S(2)}) async-start(), calls=%async_computation.2 | async-start | bytes 37748736 | tf_op jit(solution)/shard_map/all_gather | solution.py:49
  308.7 1.4 copy-start
  312.4 6.6 all-to-all-start
  319.3 3.4 copy-start.2
  319.4 5.2 copy-start.3
  319.4 7.0 copy-start.6
  319.4 8.2 copy-start.4
  319.4 8.3 copy-start.5
  1030.2 13.0 %copy-start.1 = (s32[16,16]{1,0:T(8,128)S(1)}, s32[16,16]{1,0:T(8,128)}, u32[]{:S(2)}) copy-start(s32[16,16]{1,0:T(8,128)} %param.13) | copy-start | bytes 3076
Sparse Core Ops, SparseCore 0:
  308.9 41.6 all-gather.3
